TPU v7x, 256 devices: a whole 4x4x8 slice. The times are simulated.
256 devices in a mesh: dp: 4 (over z_hi, core), ctx: 16 (over z_lo, y), tp: 4 (over x).
Axes of the slice: x: 4, y: 4, z: 8 (z_hi: 2, z_lo: 4; z = z_hi * 4 + z_lo), core: 2. Of those that a mesh axis runs over, the one named last changes fastest.
Arguments:
- teacher_part: bfloat16 [4, 4, 4096, 8192], P('dp', 'tp', 'ctx'), may hold values from -8 to 8
- student_in: bfloat16 [4, 4096, 4096], P('dp', 'ctx'), may hold values from -24 to 24
- out_proj: bfloat16 [4096, 4096], P('ctx', 'tp'), may hold values from -0.09375 to 0.09375
- segment_ids: int32 [4, 4096], P('dp'), may hold values from 0 to 7, never falling along the last dimension, each value on 1 to 1024 neighbouring positions
- valid_count: int32 [4], P('dp'), may hold values from 256 to 4096, as said below
Outputs:
- doc_loss: float32 [4], P('dp')
- wo_grad: float32 [4096, 4096], P('ctx', 'tp')
- state_grad: float32 [4, 4096, 4096], P('dp', 'ctx', 'tp')
Inputs may be any that keep to these rules, and one draw needn't show every extreme that they name: `valid_count`: one document in every draw is valid at all 4096 positions. `segment_ids`: segment numbers never fall along a document.
All inputs are finite; a program needn't handle non-finite values.
Results may differ from a plain program's by a relative error of at most 0.019.
The roundings to bfloat16 on the way count: a program that leaves them out, or rounds other values in their place, can miss the bound.
Values may be sent and summed in bfloat16 or wider, within the bound.
A program may use at most 64 MiB of HBM per device.

v0:
```python
import math
import jax
import jax.numpy as jnp
from jax import lax
from jax.sharding import PartitionSpec as P

DS = 4096
HEADS = 32
masked_score = -1e30


def shifted_2(value, axis, steps):
    count = lax.axis_size(axis)
    leading, last = (max(0, -steps), min(count, count - steps))
    return lax.ppermute(value, axis, [(source, source + steps) for source in range(leading, last)])


def log_probs(scores, allowed):
    scores = jnp.where(allowed[None, :, :], scores, masked_score)
    top = jnp.max(scores, axis=-1, keepdims=True)
    shifted = scores - top
    return shifted - jnp.log(jnp.sum(jnp.exp(shifted), axis=-1, keepdims=True))


def window_terms(
    teacher_query, teacher_keys, student_query, student_keys, allowed, live, head_count
):
    length = teacher_query.shape[0]
    teacher_qh = teacher_query.reshape(length, head_count, -1)
    teacher_kh = teacher_keys.reshape(2 * length, head_count, -1)
    student_qh = student_query.reshape(length, head_count, -1)
    student_kh = student_keys.reshape(2 * length, head_count, -1)
    teacher_scale = 1.0 / math.sqrt(teacher_qh.shape[-1])
    student_scale = 1.0 / math.sqrt(student_qh.shape[-1])
    teacher_scores = (
        jnp.einsum("qhd,khd->hqk", teacher_qh, teacher_kh, preferred_element_type=jnp.float32)
        * teacher_scale
    )
    student_scores = (
        jnp.einsum("qhd,khd->hqk", student_qh, student_kh, preferred_element_type=jnp.float32)
        * student_scale
    )
    teacher_logp = log_probs(teacher_scores, allowed)
    student_logp = log_probs(student_scores, allowed)
    teacher_prob = jnp.exp(teacher_logp)
    student_prob = jnp.exp(student_logp)
    divergence = jnp.sum(teacher_prob * (teacher_logp - student_logp), axis=-1)
    loss_part = jnp.sum(divergence * live[None, :]) / HEADS
    grad_scale = live[None, :, None] * (student_scale / HEADS)
    score_grad = ((student_prob - teacher_prob) * grad_scale).astype(jnp.bfloat16)
    query_grad = jnp.einsum(
        "hqk,khd->qhd", score_grad, student_kh, preferred_element_type=jnp.float32
    ).reshape(length, -1)
    key_grad = jnp.einsum(
        "hqk,qhd->khd", score_grad, student_qh, preferred_element_type=jnp.float32
    ).reshape(2 * length, -1)
    return (loss_part, query_grad, key_grad)


def per_device(teacher_part, student_in, out_proj, segment_ids, valid_count):
    window_len = student_in.shape[1]
    head_count = HEADS // lax.axis_size("tp")
    unscale = HEADS * math.sqrt(DS // HEADS)
    partial_sum = teacher_part[0, 0].astype(jnp.float32)
    teacher_own = lax.psum_scatter(
        partial_sum.astype(jnp.bfloat16), "tp", scatter_dimension=1, tiled=True
    )
    tokens = student_in[0]
    columns = tokens
    student_own = jnp.dot(
        columns,
        lax.all_gather(out_proj, "ctx", axis=0, tiled=True),
        preferred_element_type=jnp.float32,
    ).astype(jnp.bfloat16)
    teacher_prev, student_prev = shifted_2((teacher_own, student_own), "ctx", 1)
    teacher_keys = jnp.concatenate([teacher_prev, teacher_own], 0)
    student_keys = jnp.concatenate([student_prev, student_own], 0)
    window = lax.axis_index("ctx")
    start = window * window_len
    segments = segment_ids[0]
    segment_padded = jnp.concatenate([jnp.full((window_len,), -1, jnp.int32), segments], 0)
    query_segment = lax.dynamic_slice_in_dim(segments, start, window_len, 0)
    key_segment = lax.dynamic_slice_in_dim(segment_padded, start, 2 * window_len, 0)
    valid_limit = valid_count[0]
    query_position = start + jnp.arange(window_len, dtype=jnp.int32)
    key_position = start - window_len + jnp.arange(2 * window_len, dtype=jnp.int32)
    allowed = (key_segment[None, :] == query_segment[:, None]) & (
        key_position[None, :] < valid_limit
    )
    live = jnp.where(query_position < valid_limit, 1.0, 0.0).astype(jnp.float32)
    loss_part, query_grad, key_grad = window_terms(
        teacher_own, teacher_keys, student_own, student_keys, allowed, live, head_count
    )
    from_next = shifted_2(key_grad[:window_len].astype(jnp.bfloat16), "ctx", -1).astype(jnp.float32)
    hidden_grad = (query_grad + key_grad[window_len:] + from_next).astype(jnp.bfloat16)
    state_grad = (hidden_grad.astype(jnp.float32) * unscale)[None]
    columns = tokens
    grad_piece = lax.psum_scatter(
        jnp.einsum("tr,tc->rc", columns, hidden_grad, preferred_element_type=jnp.float32).astype(
            jnp.bfloat16
        ),
        "ctx",
        scatter_dimension=0,
        tiled=True,
    )
    wo_grad = lax.psum(grad_piece, "dp").astype(jnp.float32)
    doc_loss = lax.psum(loss_part, ("ctx", "tp"))
    return (doc_loss.reshape(1), wo_grad, state_grad)


def solution(mesh):
    return jax.shard_map(
        per_device,
        mesh=mesh,
        in_specs=(
            P("dp", "tp", "ctx", None),
            P("dp", "ctx", None),
            P("ctx", "tp"),
            P("dp", None),
            P("dp"),
        ),
        out_specs=(P("dp"), P("ctx", "tp"), P("dp", "ctx", "tp")),
        check_vma=False,
    )
```

profile of v0, /device:TPU:0, one launch (start us, length us, event | category | flops | bytes accessed | tf_op | source)
XLA Modules:
  0.0 515.2 jit_solution(8294521861776870635)
XLA Ops:
  8.1 6.5 %copy.32 = bf16[1,1,256,8192]{2,3,1,0:T(8,128)(2,1)} copy(bf16[1,1,256,8192]{3,2,1,0:T(8,128)(2,1)} %param.5) | data formatting | bytes 8388608 | tf_op args[0]
  14.6 0.5 all-gather.2.cloned.1.call-update
  15.2 50.1 %reduce-scatter.3.cloned.1.call-done = bf16[256,2048]{0,1:T(8,128)(2,1)} async-done(((bf16[256,8192]{0,1:T(8,128)(2,1)}), bf16[256,2048]{0,1:T(8,128)(2,1)}) %reduce-scatter.3.cloned.1.call-update) | async-done | bytes 1048592 | tf_op jit(solution)/shard_map/reduce_scatter | solution.py:65
  65.4 3.5 collective-permute-start
  69.6 0.2 compare_and_fusion
  69.8 44.8 %collective-permute-done = bf16[256,2048]{0,1:T(8,128)(2,1)S(1)} collective-permute-done((bf16[256,2048]{0,1:T(8,128)(2,1)}, bf16[256,2048]{0,1:T(8,128)(2,1)S(1)}, u32[]{:S(2)}, u32[]{:S(2)}) %collective-permute-start) | collective-permute-done | bytes 1048608 | tf_op jit(solution)/shard_map/ppermute | solution.py:15
  114.6 2.8 pad_maximum_fusion
  117.4 23.7 %all-gather.2.cloned.1.call-done = bf16[4096,1024]{1,0:T(8,128)(2,1)} async-done(((bf16[256,1024]{1,0:T(8,128)(2,1)}), bf16[4096,1024]{1,0:T(8,128)(2,1)}) %all-gather.2.cloned.1.call-update) | async-done | bytes 8388624 | tf_op jit(solution)/shard_map/all_gather | solution.py:72
  141.2 5.7 %fusion.24 = bf16[256,1024]{1,0:T(8,128)(2,1)S(1)} fusion(bf16[4096,1024]{1,0:T(8,128)(2,1)} %all-gather.2.cloned.1.call-done, bf16[1,256,4096]{2,1,0:T(8,128)(2,1)S(1)} %copy-done), kind=kOutput, calls=%fused_computation.32 | convolution fusion | flops 2147745792 | bytes 11010048 | tf_op jit(solution)/shard_map/dot_general | solution.py:70
  146.9 3.1 collective-permute-start.1
  150.0 5.2 %fusion.8 = f32[8,256,512]{1,2,0:T(8,128)} fusion(pred[256,512]{0,1:T(8,128)(4,1)S(1)} %compare_and_fusion, bf16[512,8,256]{0,2,1:T(8,128)(2,1)} %bitcast.58, bf16[256,8,256]{0,2,1:T(8,128)(2,1)} %bitcast.60), kind=kOutput, calls=%fused_computation.17 | convolution fusion | flops 540019200 | bytes 7471104 | tf_op jit(solution)/shard_map/sub | solution.py:21
  155.2 6.2 %log_subtract_fusion.1 = f32[8,256,512]{1,2,0:T(8,128)} fusion(f32[8,256,512]{1,2,0:T(8,128)} %fusion.8), kind=kOutput, calls=%fused_computation.6 | output fusion | flops 1051135 | bytes 8388608 | tf_op jit(solution)/shard_map/reduce_sum | solution.py:22
  161.4 1.0 copy.50
  162.4 1.0 pad_maximum_fusion.1
  163.4 1.5 copy.51
  164.9 4.3 fusion.6
  169.2 7.2 %multiply_convert_fusion = (bf16[8,256,512]{1,2,0:T(8,128)(2,1)S(1)}, f32[8,256]{1,0:T(8,128)S(1)}) fusion(f32[8,256,512]{1,2,0:T(8,128)} %log_subtract_fusion.1, f32[256]{0:T(256)S(1)} %get-tuple-element.15, f32[8,256,512]{1,2,0:T(8,128)} %fusion.6), kind=kOutput, calls=%fused_computation.8 | output fusion | flops 7340543 | bytes 10494976 | tf_op jit(solution)/shard_map/reduce_sum | solution.py:22
  176.4 1.3 copy-done.1
  177.8 0.8 convolution_bitcast_fusion
  178.6 1.3 copy-done.2
  179.9 0.9 slice.15
  180.7 2.0 copy.42
  182.8 1.5 collective-permute-start.2
  184.2 3.3 fusion.23
  187.5 1.6 copy.43
  189.1 8.7 %collective-permute-done.2 = bf16[256,1024]{1,0:T(8,128)(2,1)} collective-permute-done((bf16[256,1024]{1,0:T(8,128)(2,1)}, bf16[256,1024]{1,0:T(8,128)(2,1)}, u32[]{:S(2)}, u32[]{:S(2)}) %collective-permute-start.2) | collective-permute-done | bytes 524320 | tf_op jit(solution)/shard_map/ppermute | solution.py:15
  197.8 6.7 %convert_bitcast_fusion = bf16[4096,1024]{0,1:T(8,128)(2,1)} fusion(bf16[1,256,4096]{2,1,0:T(8,128)(2,1)S(1)} %copy-done, f32[256,1024]{1,0:T(8,128)S(1)} %copy.43, bf16[256,1024]{1,0:T(8,128)(2,1)} %collective-permute-done.2), kind=kOutput, calls=%fused_computation.4 | convolution fusion | flops 2152464384 | bytes 12058624 | tf_op jit(solution)/shard_map/tr,tc->rc/dot_general | solution.py:99
  204.6 110.2 %reduce-scatter.5.cloned.1.call-done = bf16[256,1024]{0,1:T(8,128)(2,1)} async-done(((bf16[4096,1024]{0,1:T(8,128)(2,1)}), bf16[256,1024]{0,1:T(8,128)(2,1)}) %reduce-scatter.5.cloned.1.call-update) | async-done | bytes 524304 | tf_op jit(solution)/shard_map/reduce_scatter | solution.py:98
  314.8 0.6 multiply_reduce_fusion.1
  316.1 187.3 %psum.14 = f32[1]{0:T(128)} all-reduce(f32[1]{0:T(128)} %bitcast.8), channel_id=1, replica_groups=mesh['dp'=4,'ctx'=16,'tp'=4] {'ctx','tp'}, use_global_device_ids=true, to_apply=%region_7.8 | all-reduce | flops 1 | bytes 8 | tf_op jit(solution)/shard_map/psum | solution.py:107
  503.4 2.2 multiply_bitcast_fusion
  505.5 2.2 copy.44
  (21 shorter events, 0.3 us)
Async XLA Ops:
  8.0 133.2 %copy-start = (bf16[1,256,4096]{2,1,0:T(8,128)(2,1)S(1)}, bf16[1,256,4096]{2,1,0:T(8,128)(2,1)}, u32[]{:S(2)}) copy-start(bf16[1,256,4096]{2,1,0:T(8,128)(2,1)} %param.6) | copy-start | bytes 6291460
  8.0 57.3 %reduce-scatter.3.cloned.1.call-start = ((), (), s32[]{:S(2)}) async-start(), calls=%async_computation.2 | async-start | bytes 5242880 | tf_op jit(solution)/shard_map/reduce_scatter | solution.py:65
  14.6 54.9 %copy-start.4 = (s32[1,4096]{1,0:T(1,128)S(1)}, s32[1,4096]{1,0:T(1,128)}, u32[]{:S(2)}) copy-start(s32[1,4096]{1,0:T(1,128)} %param.8) | copy-start | bytes 49156
  14.6 126.6 %all-gather.2.cloned.1.call-start = ((), (), s32[]{:S(2)}) async-start(), calls=%async_computation.3 | async-start | bytes 8912896 | tf_op jit(solution)/shard_map/all_gather | solution.py:72
  15.2 299.6 %reduce-scatter.5.cloned.1.call-start = ((), (), s32[]{:S(2)}) async-start(), calls=%async_computation.4 | async-start | bytes 8912896 | tf_op jit(solution)/shard_map/reduce_scatter | solution.py:98
  65.4 49.3 %collective-permute-start = (bf16[256,2048]{0,1:T(8,128)(2,1)}, bf16[256,2048]{0,1:T(8,128)(2,1)S(1)}, u32[]{:S(2)}, u32[]{:S(2)}) collective-permute-start(bf16[256,2048]{0,1:T(8,128)(2,1)} %reduce-scatter.3.cloned.1.call-done), channel_id=1, source_target_pairs={{0,4},{4,8},{8,12},{12,16},{16,20},{20,24},{24,28},{28,32},{32,36}... | collective-permute-start | bytes 3145736 | tf_op jit(solution)/shard_map/ppermute | solution.py:15
  146.9 15.5 %collective-permute-start.1 = (bf16[256,1024]{1,0:T(8,128)(2,1)S(1)}, bf16[256,1024]{1,0:T(8,128)(2,1)S(1)}, u32[]{:S(2)}, u32[]{:S(2)}) collective-permute-start(bf16[256,1024]{1,0:T(8,128)(2,1)S(1)} %fusion.24), channel_id=1, source_target_pairs={{0,4},{4,8},{8,12},{12,16},{16,20},{20,24},{24,28},{28,32},{32,36}... | collective-permute-start | bytes 1572872 | tf_op jit(solution)/shard_map/ppermute | solution.py:15
  169.2 8.6 %copy-start.3 = (bf16[256,1024]{0,1:T(8,128)(2,1)S(1)}, bf16[256,1024]{0,1:T(8,128)(2,1)}, u32[]{:S(2)}) copy-start(bf16[256,1024]{0,1:T(8,128)(2,1)} %copy.50) | copy-start | bytes 1572868
  176.4 1.4 copy-start.1
  178.6 1.3 copy-start.2
  182.8 15.1 %collective-permute-start.2 = (bf16[256,1024]{1,0:T(8,128)(2,1)}, bf16[256,1024]{1,0:T(8,128)(2,1)}, u32[]{:S(2)}, u32[]{:S(2)}) collective-permute-start(bf16[256,1024]{1,0:T(8,128)(2,1)} %copy.42), channel_id=1, source_target_pairs={{4,0},{8,4},{12,8},{16,12},{20,16},{24,20},{28,24},{32,28},{36,32}... | collective-permute-start | bytes 1572872 | tf_op jit(solution)/shard_map/ppermute | solution.py:15
  204.5 301.0 %all-reduce.3.cloned.1.call-start = ((), (), s32[]{:S(2)}) async-start(), calls=%async_computation.5 | async-start | bytes 1048576 | tf_op jit(solution)/shard_map/psum | solution.py:106
Sparse Core Ops, SparseCore 0:
  14.7 50.6 reduce-scatter.2
  314.9 54.1 all-reduce.2
Sparse Core Ops, SparseCore 1:
  16.9 124.3 all-gather.1
  204.6 110.1 reduce-scatter.4
where the time goes:
time: 516 us; the launch traced here: 515 us
  waiting for transfers between devices  238 us (46%)
  blocking collectives  187 us (36%)
  matrix products  25.9 us (5%)
  other arithmetic  20.2 us (4%)
  local copies, waits for them, and re-layouts  18.4 us (4%)
  between operations  16.9 us (3%)
  starting transfers between devices  8.2 us (2%)
    psum x1, blocking collectives, per_device(): doc_loss = lax.psum(loss_part, ('ctx', 'tp'))  187 us
    reduce_scatter x1, waiting for transfers between devices, per_device(): lax.psum_scatter(jnp.einsum('tr,tc->rc', columns, hidden_grad, preferred_...  110 us
    ppermute x3, waiting for transfers between devices, shifted_2(): lax.ppermute(value, axis, [(source, source + steps) for source in range(l...  53.5 us
    reduce_scatter x1, waiting for transfers between devices, per_device(): lax.psum_scatter(partial_sum.astype(jnp.bfloat16), 'tp', scatter_dimensio...  50.1 us
    all_gather x1, waiting for transfers between devices, per_device(): lax.all_gather(out_proj, 'ctx', axis=0, tiled=True)  23.7 us
    reduce_sum x2, other arithmetic, log_probs(): return shifted - jnp.log(jnp.sum(jnp.exp(shifted), axis=-1, keepdims=True))  13.4 us
    unnamed x12, local copies, waits for them, and re-layouts  11.4 us
  transfers between devices with their start and end apart: 7, of which 5 were waited for; matrix products, arithmetic and copies ran while one was open for 4% of the time, Pallas kernels for 0%

commit v1 on v0

--- a/solution.py
+++ b/solution.py
@@ -67,10 +67,12 @@
     )
     tokens = student_in[0]
     columns = tokens
+    clear_indices = lambda v0, which_axis: jnp.concatenate(
+        lax.all_to_all(jnp.stack([v0 for _ in range(lax.axis_size(which_axis))]), which_axis, 0, 0),
+        axis=0,
+    )
     student_own = jnp.dot(
-        columns,
-        lax.all_gather(out_proj, "ctx", axis=0, tiled=True),
-        preferred_element_type=jnp.float32,
+        columns, clear_indices(out_proj, "ctx"), preferred_element_type=jnp.float32
     ).astype(jnp.bfloat16)
     teacher_prev, student_prev = shifted_2((teacher_own, student_own), "ctx", 1)
     teacher_keys = jnp.concatenate([teacher_prev, teacher_own], 0)

time: 516 us -> 603 us (1.17)
  waiting for transfers between devices: 238 us -> 314 us
  starting transfers between devices: 8.2 us -> 14.5 us
    reduce_scatter x1, waiting for transfers between devices: 110 us -> 157 us  [per_device(): lax.psum_scatter(jnp.einsum('tr,tc->rc', columns, hidden_grad, preferred_...]
    all_to_all x0 -> x1, waiting for transfers between devices: none -> 36.5 us  [per_device(): lax.all_to_all(jnp.stack([v0 for _ in range(lax.axis_size(which_axis))]),...]
    all_gather x1 -> x0, waiting for transfers between devices: 23.7 us -> none  [per_device(): lax.all_gather(out_proj, 'ctx', axis=0, tiled=True)]
    ppermute x3, waiting for transfers between devices: 53.5 us -> 70.6 us  [shifted_2(): lax.ppermute(value, axis, [(source, source + steps) for source in range(l...]
    all_to_all x0 -> x1, starting transfers between devices: none -> 6.98 us  [per_device(): lax.all_to_all(jnp.stack([v0 for _ in range(lax.axis_size(which_axis))]),...]
  transfers between devices with their start and end apart: 7 -> 7, of which waited for: 5 -> 5; matrix products, arithmetic and copies ran while one was open for 4% -> 5% of each run, Pallas kernels for 0% -> 0%
where the time goes in v1:
time: 603 us; the launch traced here: 602 us
  waiting for transfers between devices  314 us (52%)
  blocking collectives  189 us (31%)
  matrix products  25.9 us (4%)
  local copies, waits for them, and re-layouts  23.8 us (4%)
  other arithmetic  20.1 us (3%)
  between operations  15.2 us (3%)
  starting transfers between devices  14.5 us (2%)
    psum x1, blocking collectives, per_device(): doc_loss = lax.psum(loss_part, ('ctx', 'tp'))  189 us
    reduce_scatter x1, waiting for transfers between devices, per_device(): lax.psum_scatter(jnp.einsum('tr,tc->rc', columns, hidden_grad, preferred_...  157 us
    ppermute x3, waiting for transfers between devices, shifted_2(): lax.ppermute(value, axis, [(source, source + steps) for source in range(l...  70.6 us
    reduce_scatter x1, waiting for transfers between devices, per_device(): lax.psum_scatter(partial_sum.astype(jnp.bfloat16), 'tp', scatter_dimensio...  49.9 us
    all_to_all x1, waiting for transfers between devices, per_device(): lax.all_to_all(jnp.stack([v0 for _ in range(lax.axis_size(which_axis))]),...  36.5 us
    reduce_sum x2, other arithmetic, log_probs(): return shifted - jnp.log(jnp.sum(jnp.exp(shifted), axis=-1, keepdims=True))  13.4 us
  transfers between devices with their start and end apart: 7, of which 5 were waited for; matrix products, arithmetic and copies ran while one was open for 5% of the time, Pallas kernels for 0%

profile of v1, /device:TPU:0, one launch (start us, length us, event | category | flops | bytes accessed | tf_op | source)
XLA Modules:
  0.0 602.0 jit_solution(9601057607871902753)
XLA Ops:
  7.2 5.5 stack.2
  12.7 7.0 %all-to-all-start = ((bf16[16,256,1024]{2,1,0:T(8,128)(2,1)}), bf16[16,256,1024]{2,1,0:T(8,128)(2,1)}, u32[]{:S(2)}, u32[]{:S(2)}) async-start(bf16[16,256,1024]{2,1,0:T(8,128)(2,1)} %stack.2), calls=%async_computation.1 | async-start | bytes 16777216 | tf_op jit(solution)/shard_map/all_to_all | solution.py:71
  19.7 6.4 %copy.32 = bf16[1,1,256,8192]{2,3,1,0:T(8,128)(2,1)} copy(bf16[1,1,256,8192]{3,2,1,0:T(8,128)(2,1)} %param.5) | data formatting | bytes 8388608 | tf_op args[0]
  26.2 49.9 %reduce-scatter.3.cloned.1.call-done = bf16[256,2048]{0,1:T(8,128)(2,1)} async-done(((bf16[256,8192]{0,1:T(8,128)(2,1)}), bf16[256,2048]{0,1:T(8,128)(2,1)}) %reduce-scatter.3.cloned.1.call-update) | async-done | bytes 1048592 | tf_op jit(solution)/shard_map/reduce_scatter | solution.py:65
  76.1 3.4 collective-permute-start
  80.6 52.7 %collective-permute-done = bf16[256,2048]{0,1:T(8,128)(2,1)S(1)} collective-permute-done((bf16[256,2048]{0,1:T(8,128)(2,1)}, bf16[256,2048]{0,1:T(8,128)(2,1)S(1)}, u32[]{:S(2)}, u32[]{:S(2)}) %collective-permute-start) | collective-permute-done | bytes 1048608 | tf_op jit(solution)/shard_map/ppermute | solution.py:15
  133.3 2.7 pad_maximum_fusion
  136.0 36.5 %all-to-all-done = bf16[16,256,1024]{2,1,0:T(8,128)(2,1)} async-done(((bf16[16,256,1024]{2,1,0:T(8,128)(2,1)}), bf16[16,256,1024]{2,1,0:T(8,128)(2,1)}, u32[]{:S(2)}, u32[]{:S(2)}) %all-to-all-start) | async-done | bytes 8388640 | tf_op jit(solution)/shard_map/all_to_all | solution.py:71
  172.5 5.7 fusion.24
  178.2 2.5 collective-permute-start.1
  180.7 5.2 fusion.8
  185.8 6.2 %log_subtract_fusion.1 = f32[8,256,512]{1,2,0:T(8,128)} fusion(f32[8,256,512]{1,2,0:T(8,128)} %fusion.8), kind=kOutput, calls=%fused_computation.6 | output fusion | flops 1051135 | bytes 8388608 | tf_op jit(solution)/shard_map/reduce_sum | solution.py:22
  192.1 1.0 copy.50
  193.1 1.0 pad_maximum_fusion.1
  194.1 1.5 copy.51
  195.6 4.3 fusion.6
  199.9 7.2 %multiply_convert_fusion = (bf16[8,256,512]{1,2,0:T(8,128)(2,1)S(1)}, f32[8,256]{1,0:T(8,128)S(1)}) fusion(f32[8,256,512]{1,2,0:T(8,128)} %log_subtract_fusion.1, f32[256]{0:T(256)S(1)} %get-tuple-element.15, f32[8,256,512]{1,2,0:T(8,128)} %fusion.6), kind=kOutput, calls=%fused_computation.8 | output fusion | flops 7340543 | bytes 10494976 | tf_op jit(solution)/shard_map/reduce_sum | solution.py:22
  207.1 1.3 copy-done.1
  208.4 0.8 convolution_bitcast_fusion
  209.2 1.3 copy-done.2
  210.5 0.9 slice.15
  211.4 2.0 copy.42
  213.4 1.5 collective-permute-start.2
  214.9 3.3 fusion.23
  218.2 1.6 copy.43
  219.8 17.9 %collective-permute-done.2 = bf16[256,1024]{1,0:T(8,128)(2,1)} collective-permute-done((bf16[256,1024]{1,0:T(8,128)(2,1)}, bf16[256,1024]{1,0:T(8,128)(2,1)}, u32[]{:S(2)}, u32[]{:S(2)}) %collective-permute-start.2) | collective-permute-done | bytes 524320 | tf_op jit(solution)/shard_map/ppermute | solution.py:15
  237.6 6.7 %convert_bitcast_fusion = bf16[4096,1024]{0,1:T(8,128)(2,1)} fusion(bf16[1,256,4096]{2,1,0:T(8,128)(2,1)S(1)} %copy-done, f32[256,1024]{1,0:T(8,128)S(1)} %copy.43, bf16[256,1024]{1,0:T(8,128)(2,1)} %collective-permute-done.2), kind=kOutput, calls=%fused_computation.4 | convolution fusion | flops 2152464384 | bytes 12058624 | tf_op jit(solution)/shard_map/tr,tc->rc/dot_general | solution.py:101
  244.4 156.7 %reduce-scatter.5.cloned.1.call-done = bf16[256,1024]{0,1:T(8,128)(2,1)} async-done(((bf16[4096,1024]{0,1:T(8,128)(2,1)}), bf16[256,1024]{0,1:T(8,128)(2,1)}) %reduce-scatter.5.cloned.1.call-update) | async-done | bytes 524304 | tf_op jit(solution)/shard_map/reduce_scatter | solution.py:100
  401.1 0.6 multiply_reduce_fusion.1
  402.4 188.7 %psum.14 = f32[1]{0:T(128)} all-reduce(f32[1]{0:T(128)} %bitcast.9), channel_id=1, replica_groups=mesh['dp'=4,'ctx'=16,'tp'=4] {'ctx','tp'}, use_global_device_ids=true, to_apply=%region_7.8 | all-reduce | flops 1 | bytes 8 | tf_op jit(solution)/shard_map/psum | solution.py:109
  591.1 2.2 multiply_bitcast_fusion
  593.3 2.2 copy.44
  (21 shorter events, 0.5 us)
Async XLA Ops:
  7.2 165.3 %copy-start = (bf16[1,256,4096]{2,1,0:T(8,128)(2,1)S(1)}, bf16[1,256,4096]{2,1,0:T(8,128)(2,1)}, u32[]{:S(2)}) copy-start(bf16[1,256,4096]{2,1,0:T(8,128)(2,1)} %param.6) | copy-start | bytes 6291460
  12.7 159.8 %all-to-all-start = ((bf16[16,256,1024]{2,1,0:T(8,128)(2,1)}), bf16[16,256,1024]{2,1,0:T(8,128)(2,1)}, u32[]{:S(2)}, u32[]{:S(2)}) async-start(bf16[16,256,1024]{2,1,0:T(8,128)(2,1)} %stack.2), calls=%async_computation.1 | async-start | bytes 16777216 | tf_op jit(solution)/shard_map/all_to_all | solution.py:71
  19.6 56.5 %reduce-scatter.3.cloned.1.call-start = ((), (), s32[]{:S(2)}) async-start(), calls=%async_computation.3 | async-start | bytes 5242880 | tf_op jit(solution)/shard_map/reduce_scatter | solution.py:65
  26.1 54.1 %copy-start.4 = (s32[1,4096]{1,0:T(1,128)S(1)}, s32[1,4096]{1,0:T(1,128)}, u32[]{:S(2)}) copy-start(s32[1,4096]{1,0:T(1,128)} %param.8) | copy-start | bytes 49156
  26.1 375.0 %reduce-scatter.5.cloned.1.call-start = ((), (), s32[]{:S(2)}) async-start(), calls=%async_computation.4 | async-start | bytes 8912896 | tf_op jit(solution)/shard_map/reduce_scatter | solution.py:100
  76.1 57.2 %collective-permute-start = (bf16[256,2048]{0,1:T(8,128)(2,1)}, bf16[256,2048]{0,1:T(8,128)(2,1)S(1)}, u32[]{:S(2)}, u32[]{:S(2)}) collective-permute-start(bf16[256,2048]{0,1:T(8,128)(2,1)} %reduce-scatter.3.cloned.1.call-done), channel_id=1, source_target_pairs={{0,4},{4,8},{8,12},{12,16},{16,20},{20,24},{24,28},{28,32},{32,36}... | collective-permute-start | bytes 3145736 | tf_op jit(solution)/shard_map/ppermute | solution.py:15
  178.2 14.8 %collective-permute-start.1 = (bf16[256,1024]{1,0:T(8,128)(2,1)S(1)}, bf16[256,1024]{1,0:T(8,128)(2,1)S(1)}, u32[]{:S(2)}, u32[]{:S(2)}) collective-permute-start(bf16[256,1024]{1,0:T(8,128)(2,1)S(1)} %fusion.24), channel_id=1, source_target_pairs={{0,4},{4,8},{8,12},{12,16},{16,20},{20,24},{24,28},{28,32},{32,36}... | collective-permute-start | bytes 1572872 | tf_op jit(solution)/shard_map/ppermute | solution.py:15
  199.9 8.6 %copy-start.3 = (bf16[256,1024]{0,1:T(8,128)(2,1)S(1)}, bf16[256,1024]{0,1:T(8,128)(2,1)}, u32[]{:S(2)}) copy-start(bf16[256,1024]{0,1:T(8,128)(2,1)} %copy.50) | copy-start | bytes 1572868
  207.1 1.4 copy-start.1
  209.2 1.3 copy-start.2
  213.4 24.2 %collective-permute-start.2 = (bf16[256,1024]{1,0:T(8,128)(2,1)}, bf16[256,1024]{1,0:T(8,128)(2,1)}, u32[]{:S(2)}, u32[]{:S(2)}) collective-permute-start(bf16[256,1024]{1,0:T(8,128)(2,1)} %copy.42), channel_id=1, source_target_pairs={{4,0},{8,4},{12,8},{16,12},{20,16},{24,20},{28,24},{32,28},{36,32}... | collective-permute-start | bytes 1572872 | tf_op jit(solution)/shard_map/ppermute | solution.py:15
  244.3 349.0 %all-reduce.3.cloned.1.call-start = ((), (), s32[]{:S(2)}) async-start(), calls=%async_computation.5 | async-start | bytes 1048576 | tf_op jit(solution)/shard_map/psum | solution.py:108
Sparse Core Ops, SparseCore 0:
  26.2 49.8 reduce-scatter.2
  244.4 156.6 reduce-scatter.4
  403.8 54.1 all-reduce.2
